TPU v7x, 32 devices: a whole 2x2x4 slice. The times are simulated.
32 devices in a mesh: groups: 2 (over x), beam: 16 (over z, y, core).
Axes of the slice: x: 2, y: 2, z: 4, core: 2. Of those that a mesh axis runs over, the one named last changes fastest.
Arguments:
- transmission: float32 [2, 2, 512, 512], P('groups'), parts along dimension 0, may hold values from -1 to 1, as said below
- beams: int32 [16, 2], P('beam'), may hold values from -64 to 63
- phases: int32 [32, 16], replicated, may hold values from 0 to 63
- positions: int32 [32, 2], replicated, may hold values from 0 to 128
- owner: int32 [32], replicated, may hold values from 0 to 15, as said below
Outputs:
- patterns: float32 [128, 128, 128], P(('groups', 'beam')), parts along dimension 0
There are 2 independent parts, one for each index of `groups`. A program takes and returns all parts, laid end to end along the dimension named above; an argument that names none is the same for every part. Nothing has to cross between parts.
Inputs may be any that keep to these rules, and one draw needn't show every extreme that they name: `transmission`: real and imaginary parts of each pixel form a pair of magnitude at most 1. Each owner is given at most 4 probes, and some owner exactly 4.
All inputs are finite; a program needn't handle non-finite values.
Results may differ from a plain program's by a relative error of at most 0.0003.
Values sent between devices are 32-bit elements; how exact they have to be, the bound alone decides.
No kernel may reach another device: no remote copies, remote signals or barrier semaphores. Data moves between devices by JAX's collectives and lax.ppermute only.
A program may use at most 64 MiB of HBM per device.

v0:
```python
import math

import jax
import jax.numpy as jnp
import numpy as np
from jax import lax
from jax.experimental import pallas as pl
from jax.experimental.pallas import tpu as pltpu
from jax.sharding import PartitionSpec as P


CROP = 256
WINDOW = 128
LEVELS = 64
CAP = 4
SPAN = CROP - WINDOW
VMEM_LIMIT = 40 << 20
STEP = 32
WIDE = 256

prop_rate = 0.0004 * math.pi
two_pi = 2.0 * math.pi


def window_operator(length):
    index = np.arange(length)
    freq = np.where(index < length // 2, index, index - length)
    kernel = np.fft.ifft(np.exp(-1j * prop_rate * freq.astype(np.float64) ** 2))
    lower = (length - CROP) // 2
    rows = np.arange(-SPAN, length + 8)
    point = np.arange(WINDOW)
    shifted = kernel[(lower + point[None, :] - rows[:, None]) % length]
    wave = np.exp(-1j * two_pi * (point[:, None] * point[None, :] % WINDOW) / WINDOW)
    table = shifted @ wave / math.sqrt(WINDOW)
    return np.concatenate([table.real, table.imag], axis=1).astype(np.float32)


def row_operator(table):
    rows = table[SPAN : table.shape[0] - 8].T
    high = rows.astype(jnp.bfloat16)
    low = (rows - high.astype(np.float32)).astype(jnp.bfloat16)
    return np.concatenate([high, high, low], axis=1)


def partners(count):
    return [1 << bit | 1 for bit in range(1, count.bit_length() - 1)] + [1]


def split(value):
    high = value.astype(jnp.bfloat16)
    return high, (value - high.astype(jnp.float32)).astype(jnp.bfloat16)


def dot(left, right):
    return jnp.dot(left, right, preferred_element_type=jnp.float32)


def moved(table_ref, start, length):
    whole = start // 8
    rest = start - whole * 8
    width = table_ref.shape[1]
    rows = table_ref[pl.ds(pl.multiple_of(whole * 8, 8), length + 8), :].reshape(length // 8 + 1, 8, width)
    rows = pltpu.roll(rows, jnp.where(rest == 0, 0, 8 - rest), axis=1)
    inside = lax.broadcasted_iota(jnp.int32, (1, 8, width), 1) < 8 - rest
    return jnp.where(inside, rows[:-1], rows[1:]).reshape(length, width)


def pick_kernel(owner_hbm, position_hbm, phase_hbm, weight_ref, offset_ref, owner_ref, position_ref, phase_ref, pick_ref, sems):
    slots, (beams, probes) = weight_ref.shape[0], phase_ref.shape
    pairs = [(owner_hbm, owner_ref), (position_hbm, position_ref), (phase_hbm, phase_ref)]
    copies = [pltpu.make_async_copy(*pair, sems.at[index]) for index, pair in enumerate(pairs)]
    for copy in copies:
        copy.start()
    me = lax.axis_index("beam")
    for slot in range(slots):
        pick_ref[slot] = -1
    lane = lax.broadcasted_iota(jnp.int32, (beams, probes), 1)
    row = lax.broadcasted_iota(jnp.int32, (beams, 128), 0)
    column = lax.broadcasted_iota(jnp.int32, (beams, 128), 1)
    flips = jnp.zeros_like(column)
    for step, mask in enumerate(partners(beams)):
        flips = flips ^ jnp.where((column >> step & 1) == 1, mask, 0)
    copies[0].wait()

    def visit(probe, count):
        hit = owner_ref[probe] == me
        pick_ref[jnp.where(hit, count, slots)] = probe
        return count + jnp.where(hit, 1, 0)

    lax.fori_loop(0, probes, visit, 0)
    for copy in copies[1:]:
        copy.wait()
    for slot in range(slots):
        pick = pick_ref[slot]
        level = jnp.sum(jnp.where(lane == pick, phase_ref[...], 0), axis=1, keepdims=True)
        level = jnp.sum(jnp.where(row == flips ^ me, level, 0), axis=0, keepdims=True)
        level = jnp.sum(jnp.where(row == column, level, 0), axis=1, keepdims=True)
        level = jnp.broadcast_to(level, (beams, 128))
        scale = jnp.where(pick >= 0, 1.0 / math.sqrt(beams), 0.0)
        weight_ref[slot, 0] = cosine(level, LEVELS) * scale
        weight_ref[slot, 1] = cosine(level - LEVELS // 4, LEVELS) * scale
        probe = jnp.maximum(pick, 0)
        offset_ref[2 * slot] = position_ref[0, probe]
        offset_ref[2 * slot + 1] = position_ref[1, probe]


def fetch_kernel(specimen_hbm, specimen_ref, sem):
    copy = pltpu.make_async_copy(specimen_hbm.at[0, :, :, 0 : specimen_ref.shape[2]], specimen_ref, sem)
    copy.start()
    copy.wait()


def place_kernel(offset_hbm, table_hbm, right_ref, offset_ref, table_ref, sems):
    slots, length = right_ref.shape[0], right_ref.shape[2]
    copies = [
        pltpu.make_async_copy(table_hbm, table_ref, sems.at[0]),
        pltpu.make_async_copy(offset_hbm, offset_ref, sems.at[1]),
    ]
    for copy in copies:
        copy.start()
    for copy in copies:
        copy.wait()
    for slot in range(slots):
        cols = moved(table_ref, SPAN - offset_ref[2 * slot + 1], length)
        right_ref[slot, 0], right_ref[slot, 1] = split(cols)


def cosine(turns, length):
    quarter = length // 4
    shift = quarter.bit_length() - 1
    turns = turns & (length - 1)
    quadrant = (turns + quarter // 2) >> shift
    angle = (turns - (quadrant << shift)).astype(jnp.float32) * (two_pi / length)
    square = angle * angle
    even = 1.0 + square * (-1.0 / 2 + square * (1.0 / 24 + square * (-1.0 / 720 + square * (1.0 / 40320))))
    odd = angle * (1.0 + square * (-1.0 / 6 + square * (1.0 / 120 + square * (-1.0 / 5040))))
    value = jnp.where((quadrant & 1) == 0, even, odd)
    return jnp.where(((quadrant + 1) & 2) == 0, value, -value)


def probe_kernel(
    beam_ref,
    weight_ref,
    near_ref,
    right_ref,
    offset_ref,
    transmission_hbm,
    left_hbm,
    out_hbm,
    far_ref,
    left_ref,
    row_ref,
    col_ref,
    mix_ref,
    light_ref,
    lit_ref,
    half_ref,
    out_ref,
    start_ref,
    sems,
    out_sems,
):
    slots, length = out_ref.shape[0], transmission_hbm.shape[-1]
    beams = beam_ref.shape[0]
    depth = row_ref.shape[1]
    quarter = length // 4
    copy = pltpu.make_async_copy(offset_ref, start_ref, sems.at[0])
    copy.start()
    far = pltpu.make_async_copy(transmission_hbm.at[0, :, :, length // 2 :], far_ref, sems.at[2])
    far.start()
    left = pltpu.make_async_copy(left_hbm, left_ref, sems.at[1])
    left.start()
    row_freq = beam_ref[:, 0, 0:128]
    col_freq = beam_ref[:, 0, 128:256]
    lane = lax.broadcasted_iota(jnp.int32, (beams, depth), 1)
    member = lax.broadcasted_iota(jnp.int32, (beams, depth), 0)
    wide = jnp.concatenate([row_freq] * (depth // 128), axis=1)
    freq = jnp.sum(jnp.where(lane % beams == member, wide, 0), axis=0, keepdims=True)
    block = lax.broadcasted_iota(jnp.int32, (1, depth), 1) // beams
    shift = jnp.where(block % 2 == 1, quarter, 0)
    fine = lax.broadcasted_iota(jnp.int32, (STEP, depth), 0) * freq
    fine_cos, fine_sin = cosine(fine, length), cosine(fine - quarter, length)
    coarse = lax.broadcasted_iota(jnp.int32, (length // STEP, depth), 0) * (STEP * freq) - shift
    coarse_cos, coarse_sin = cosine(coarse, length), cosine(coarse - quarter, length)
    for index in range(length // STEP):
        waves = coarse_cos[index : index + 1] * fine_cos - coarse_sin[index : index + 1] * fine_sin
        high = waves.astype(jnp.bfloat16).astype(jnp.float32)
        parts = jnp.where(block < 4, high, jnp.where(block < 6, waves - high, 0.0))
        row_ref[index * STEP : (index + 1) * STEP] = parts.astype(jnp.bfloat16)
    pixel = lax.broadcasted_iota(jnp.int32, (beams, length), 1)
    turns = pixel * jnp.concatenate([col_freq] * (length // 128), axis=1)
    col_ref[0] = cosine(turns, length)
    col_ref[1] = cosine(turns - quarter, length)
    if depth > 6 * beams:
        for way in range(mix_ref.shape[0]):
            mix_ref[way, 6 * beams :] = jnp.zeros((depth - 6 * beams, 2 * length), jnp.bfloat16)

    def light(slot, way):
        weight_real = jnp.concatenate([weight_ref[slot, 0]] * (length // 128), axis=1)
        weight_imag = jnp.concatenate([weight_ref[slot, 1]] * (length // 128), axis=1)
        real = weight_real * col_ref[0] - weight_imag * col_ref[1]
        imag = weight_real * col_ref[1] + weight_imag * col_ref[0]
        tiles = [slice(start, start + 128) for start in range(0, length, 128)]
        for_cos = split(jnp.concatenate([x[:, tile] for tile in tiles for x in (real, imag)], axis=1))
        for_sin = split(jnp.concatenate([x[:, tile] for tile in tiles for x in (-imag, real)], axis=1))
        parts = [for_cos[0], for_sin[0], for_cos[1], for_sin[1], for_cos[0], for_sin[0]]
        for index, part in enumerate(parts):
            mix_ref[way, index * beams : (index + 1) * beams] = part

    def light_tile(tile, way):
        light_ref[way, tile] = dot(row_ref[...], mix_ref[way, :, tile * 256 : (tile + 1) * 256])

    def shine(tile, way):
        specimen_ref = near_ref if tile * 128 < length // 2 else far_ref
        cols = slice(tile * 128 % (length // 2), tile * 128 % (length // 2) + 128)
        stretch, start = tile * 128 // WIDE, tile * 128 % WIDE
        lanes = slice(start, start + 128)
        for row in range(0, length, 32):
            rows = slice(row, row + 32)
            light_real, light_imag = light_ref[way, tile, rows, 0:128], light_ref[way, tile, rows, 128:256]
            real, imag = specimen_ref[0, rows, cols], specimen_ref[1, rows, cols]
            high, low = split(real * light_real - imag * light_imag)
            lit_ref[way, stretch, 0, rows, lanes], lit_ref[way, stretch, 1, rows, lanes] = high, low
            high, low = split(real * light_imag + imag * light_real)
            lit_ref[way, length // WIDE + stretch, 0, rows, lanes], lit_ref[way, length // WIDE + stretch, 1, rows, lanes] = high, low

    def along_cols(slot, way):
        source, operator = [], []
        for stretch in range(2 * length // WIDE):
            rows = slice(stretch * WIDE % length, stretch * WIDE % length + WIDE)
            high, low = right_ref[slot, 0, rows], right_ref[slot, 1, rows]
            if stretch * WIDE >= length:
                high, low = (jnp.concatenate([-x[:, WINDOW:], x[:, :WINDOW]], axis=1) for x in (high, low))
            source += [lit_ref[way, stretch, 0], lit_ref[way, stretch, 0], lit_ref[way, stretch, 1]]
            operator += [high, low, high]
        half = dot(jnp.concatenate(source, axis=1), jnp.concatenate(operator, axis=0))
        half_ref[way, 0:length] = half
        half_ref[way, length:] = half[0 : SPAN + 8]

    def along_rows(slot, way):
        high, low = split(moved(half_ref.at[way], start_ref[2 * slot], length))
        full = dot(left_ref[...], jnp.concatenate([high, low, high], axis=0))
        real = full[:WINDOW, :WINDOW] - full[WINDOW:, WINDOW:]
        imag = full[:WINDOW, WINDOW:] + full[WINDOW:, :WINDOW]
        out_ref[slot] = real * real + imag * imag
        pltpu.make_async_copy(out_ref.at[slot], out_hbm.at[slot], out_sems.at[slot]).start()

    def prepare(slot):
        light(slot, slot)
        light_tile(0, slot)
        for tile in range(1, length // 128):
            light_tile(tile, slot)
            if slot == 0 and tile == length // 256 + 1:
                far.wait()
            shine(tile - 1, slot)
        shine(length // 128 - 1, slot)

    prepare(0)
    for slot in range(slots):
        along_cols(slot, slot)
        if slot + 1 < slots:
            prepare(slot + 1)
    copy.wait()
    left.wait()
    for slot in range(slots):
        along_rows(slot, slot)
    for slot in range(slots):
        pltpu.make_async_copy(out_ref.at[slot], out_hbm.at[slot], out_sems.at[slot]).wait()


def probe_call(every, weight, specimen, right, offset, transmission, left):
    length = transmission.shape[-1]
    depth = pl.cdiv(6 * every.shape[0], 128) * 128
    weight, specimen, right = (pltpu.with_memory_space_constraint(x, pltpu.VMEM) for x in (weight, specimen, right))
    transmission, left = (pltpu.with_memory_space_constraint(x, pltpu.HBM) for x in (transmission, left))
    vmem = pl.BlockSpec(memory_space=pltpu.VMEM)
    anywhere = pl.BlockSpec(memory_space=pltpu.HBM)
    return pl.pallas_call(
        probe_kernel,
        out_shape=jax.ShapeDtypeStruct((CAP, WINDOW, WINDOW), jnp.float32),
        in_specs=[vmem] * 4 + [pl.BlockSpec(memory_space=pl.ANY)] + [anywhere] * 2,
        out_specs=anywhere,
        scratch_shapes=[
            pltpu.VMEM(specimen.shape, specimen.dtype),
            pltpu.VMEM(left.shape, left.dtype),
            pltpu.VMEM((length, depth), jnp.bfloat16),
            pltpu.VMEM((2, every.shape[0], length), jnp.float32),
            pltpu.VMEM((CAP, depth, 2 * length), jnp.bfloat16),
            pltpu.VMEM((CAP, length // 128, length, 256), jnp.float32),
            pltpu.VMEM((CAP, 2 * length // WIDE, 2, length, WIDE), jnp.bfloat16),
            pltpu.VMEM((CAP, length + SPAN + 8, 2 * WINDOW), jnp.float32),
            pltpu.VMEM((CAP, WINDOW, WINDOW), jnp.float32),
            pltpu.SMEM((2 * CAP,), jnp.int32),
            pltpu.SemaphoreType.DMA((3,)),
            pltpu.SemaphoreType.DMA((CAP,)),
        ],
        compiler_params=pltpu.CompilerParams(vmem_limit_bytes=VMEM_LIMIT),
        name="probes",
    )(every, weight, specimen, right, offset, transmission, left)


def local(transmission, beams, phases, positions, owner):
    length = transmission.shape[-1]
    beam_count = lax.axis_size("beam")
    beam_total = phases.shape[1]
    every = jnp.broadcast_to(beams[:, :, None], (1, 2, 128)).reshape(1, 1, 256)
    for mask in partners(beam_count):
        pairs = [(here, here ^ mask) for here in range(beam_count)]
        other = lax.ppermute(every, "beam", pairs)
        every = jnp.concatenate([every, other], axis=0)
    vmem = pl.BlockSpec(memory_space=pltpu.VMEM)
    smem = pl.BlockSpec(memory_space=pltpu.SMEM)
    anywhere = pl.BlockSpec(memory_space=pltpu.HBM)
    params = pltpu.CompilerParams(vmem_limit_bytes=VMEM_LIMIT)
    weight, offset = pl.pallas_call(
        pick_kernel,
        out_shape=(
            pltpu.VMEM((CAP, 2, beam_total, 128), jnp.float32),
            jax.ShapeDtypeStruct((2 * CAP,), jnp.int32),
        ),
        in_specs=[anywhere] * 3,
        out_specs=(vmem, smem),
        scratch_shapes=[
            pltpu.SMEM(owner.shape, jnp.int32),
            pltpu.SMEM(positions.shape[::-1], jnp.int32),
            pltpu.VMEM(phases.shape[::-1], jnp.int32),
            pltpu.SMEM((CAP + 1,), jnp.int32),
            pltpu.SemaphoreType.DMA((3,)),
        ],
        compiler_params=params,
        name="pick",
    )(*(pltpu.with_memory_space_constraint(x, pltpu.HBM) for x in (owner, positions.T, phases.T)))
    specimen = pl.pallas_call(
        fetch_kernel,
        out_shape=pltpu.VMEM((2, length, length // 2), jnp.float32),
        in_specs=[anywhere],
        out_specs=vmem,
        scratch_shapes=[pltpu.SemaphoreType.DMA],
        compiler_params=params,
        name="fetch",
    )(pltpu.with_memory_space_constraint(transmission, pltpu.HBM))
    table = window_operator(length)
    right = pl.pallas_call(
        place_kernel,
        out_shape=pltpu.VMEM((CAP, 2, length, 2 * WINDOW), jnp.bfloat16),
        in_specs=[pl.BlockSpec(memory_space=pl.ANY), anywhere],
        out_specs=vmem,
        scratch_shapes=[
            pltpu.SMEM((2 * CAP,), jnp.int32),
            pltpu.VMEM(table.shape, jnp.float32),
            pltpu.SemaphoreType.DMA((2,)),
        ],
        compiler_params=params,
        name="place",
    )(offset, pltpu.with_memory_space_constraint(jnp.asarray(table), pltpu.HBM))
    return probe_call(every, weight, specimen, right, offset, transmission, jnp.asarray(row_operator(table)))


def solution(mesh):
    in_specs = (P("groups", None, None, None), P("beam", None), P(), P(), P())
    out_specs = P(("groups", "beam"), None, None)
    return jax.shard_map(local, mesh=mesh, in_specs=in_specs, out_specs=out_specs, check_vma=False)
```

profile of v0, /device:TPU:0, one launch (start us, length us, event | category | flops | bytes accessed | tf_op | source)
XLA Modules:
  0.0 24.6 jit_solution(2467676880725951056)
XLA Ops:
  0.0 0.7 %broadcast_in_dim.11 = s32[2,128]{1,0:T(2,128)S(1)} broadcast(s32[2]{0:T(128)} %bitcast.11), dimensions={0} | broadcast | bytes 1032 | tf_op jit(solution)/shard_map/broadcast_in_dim | solution.py:306
  0.7 2.4 %collective-permute-start = (s32[1,1,256]{2,1,0:T(1,128)S(1)}, s32[1,1,256]{2,1,0:T(1,128)S(1)}, u32[]{:S(2)}, u32[]{:S(2)}) collective-permute-start(s32[1,1,256]{2,1,0:T(1,128)S(1)} %bitcast.4), channel_id=1, source_target_pairs={{0,3},{1,2},{2,1},{3,0},{4,7},{5,6},{6,5},{7,4},{8,11},{9,10},{10,... | collective-permute-start | bytes 3080 | tf_op jit(solution)/shard_map/ppermute | solution.py:309
  3.2 1.2 %fetch.1.near_ref = f32[2,512,256]{2,1,0:T(8,128)S(1)} custom-call(f32[1,2,512,512]{3,2,1,0:T(8,128)} %transmission_hbm.1), custom_call_target="tpu_custom_call" | custom-call | tf_op jit(solution)/shard_map/fetch/pallas_call | solution.py:333
  4.4 1.8 %pick.1 = (f32[4,2,16,128]{3,2,1,0:T(8,128)S(1)}, s32[8]{0:T(128)S(1)}) custom-call(s32[32]{0:T(128)} %owner_hbm.1, s32[2,32]{1,0:T(2,128)} %bitcast.10, s32[16,32]{1,0:T(8,128)} %bitcast.9), custom_call_target="tpu_custom_call" | custom-call | tf_op jit(solution)/shard_map/pick/pallas_call | solution.py:315
  6.3 1.6 %place.1.right_ref = bf16[4,2,512,256]{3,2,1,0:T(8,128)(2,1)S(1)} custom-call(s32[8]{0:T(128)S(1)} %get-tuple-element.8.offset_hbm.offset_ref, f32[648,256]{1,0:T(8,128)} %constant.4.clone.table_hbm), custom_call_target="tpu_custom_call" | custom-call | tf_op jit(solution)/shard_map/place/pallas_call | solution.py:343
  7.8 0.0 collective-permute-done
  7.8 1.9 %collective-permute-start.1 = (s32[2,1,256]{2,1,0:T(1,128)S(1)}, s32[2,1,256]{2,1,0:T(1,128)S(1)}, u32[]{:S(2)}, u32[]{:S(2)}) collective-permute-start(s32[2,1,256]{2,1,0:T(1,128)S(1)} %pad_add_fusion.2), channel_id=1, source_target_pairs={{0,5},{1,4},{2,7},{3,6},{4,1},{5,0},{6,3},{7,2},{8,13},{9,12},{10,... | collective-permute-start | bytes 6152 | tf_op jit(solution)/shard_map/ppermute | solution.py:309
  9.8 1.3 %collective-permute-done.1 = s32[2,1,256]{2,1,0:T(1,128)S(1)} collective-permute-done((s32[2,1,256]{2,1,0:T(1,128)S(1)}, s32[2,1,256]{2,1,0:T(1,128)S(1)}, u32[]{:S(2)}, u32[]{:S(2)}) %collective-permute-start.1) | collective-permute-done | bytes 2080 | tf_op jit(solution)/shard_map/ppermute | solution.py:309
  11.1 2.7 %collective-permute-start.2 = (s32[4,1,256]{2,1,0:T(1,128)S(1)}, s32[4,1,256]{2,1,0:T(1,128)S(1)}, u32[]{:S(2)}, u32[]{:S(2)}) collective-permute-start(s32[4,1,256]{2,1,0:T(1,128)S(1)} %pad_add_fusion.1), channel_id=1, source_target_pairs={{0,9},{1,8},{2,11},{3,10},{4,13},{5,12},{6,15},{7,14},{8,1},{9,0},... | collective-permute-start | bytes 12296 | tf_op jit(solution)/shard_map/ppermute | solution.py:309
  13.8 1.3 %collective-permute-done.2 = s32[4,1,256]{2,1,0:T(1,128)S(1)} collective-permute-done((s32[4,1,256]{2,1,0:T(1,128)S(1)}, s32[4,1,256]{2,1,0:T(1,128)S(1)}, u32[]{:S(2)}, u32[]{:S(2)}) %collective-permute-start.2) | collective-permute-done | bytes 4128 | tf_op jit(solution)/shard_map/ppermute | solution.py:309
  15.1 0.4 %collective-permute-start.3 = (s32[8,1,256]{2,1,0:T(1,128)S(1)}, s32[8,1,256]{2,1,0:T(1,128)S(1)}, u32[]{:S(2)}, u32[]{:S(2)}) collective-permute-start(s32[8,1,256]{2,1,0:T(1,128)S(1)} %pad_add_fusion), channel_id=1, source_target_pairs={{0,1},{1,0},{2,3},{3,2},{4,5},{5,4},{6,7},{7,6},{8,9},{9,8},{10,11... | collective-permute-start | bytes 24584 | tf_op jit(solution)/shard_map/ppermute | solution.py:309
  15.5 0.8 %collective-permute-done.3 = s32[8,1,256]{2,1,0:T(1,128)S(1)} collective-permute-done((s32[8,1,256]{2,1,0:T(1,128)S(1)}, s32[8,1,256]{2,1,0:T(1,128)S(1)}, u32[]{:S(2)}, u32[]{:S(2)}) %collective-permute-start.3) | collective-permute-done | bytes 8224 | tf_op jit(solution)/shard_map/ppermute | solution.py:309
  16.4 8.3 %probes.1 = f32[4,128,128]{2,1,0:T(8,128)} custom-call(s32[16,1,256]{2,1,0:T(1,128)S(1)} %constant_dynamic-update-slice_fusion.beam_ref, f32[4,2,16,128]{3,2,1,0:T(8,128)S(1)} %get-tuple-element.7.weight_ref, f32[2,512,256]{2,1,0:T(8,128)S(1)} %fetch.1.near_ref, bf16[4,2,512,256]{3,2,1,0:T(8,128)(2,1)S(1)} %place.1.right_ref, ...), custom_call_target="tpu_custom_call" | custom-call | tf_op jit(solution)/shard_map/probes/pallas_call | solution.py:278
  (8 shorter events, 0.0 us)
Async XLA Ops:
  0.7 7.1 %collective-permute-start = (s32[1,1,256]{2,1,0:T(1,128)S(1)}, s32[1,1,256]{2,1,0:T(1,128)S(1)}, u32[]{:S(2)}, u32[]{:S(2)}) collective-permute-start(s32[1,1,256]{2,1,0:T(1,128)S(1)} %bitcast.4), channel_id=1, source_target_pairs={{0,3},{1,2},{2,1},{3,0},{4,7},{5,6},{6,5},{7,4},{8,11},{9,10},{10,... | collective-permute-start | bytes 3080 | tf_op jit(solution)/shard_map/ppermute | solution.py:309
  7.8 3.2 %collective-permute-start.1 = (s32[2,1,256]{2,1,0:T(1,128)S(1)}, s32[2,1,256]{2,1,0:T(1,128)S(1)}, u32[]{:S(2)}, u32[]{:S(2)}) collective-permute-start(s32[2,1,256]{2,1,0:T(1,128)S(1)} %pad_add_fusion.2), channel_id=1, source_target_pairs={{0,5},{1,4},{2,7},{3,6},{4,1},{5,0},{6,3},{7,2},{8,13},{9,12},{10,... | collective-permute-start | bytes 6152 | tf_op jit(solution)/shard_map/ppermute | solution.py:309
  11.1 4.0 %collective-permute-start.2 = (s32[4,1,256]{2,1,0:T(1,128)S(1)}, s32[4,1,256]{2,1,0:T(1,128)S(1)}, u32[]{:S(2)}, u32[]{:S(2)}) collective-permute-start(s32[4,1,256]{2,1,0:T(1,128)S(1)} %pad_add_fusion.1), channel_id=1, source_target_pairs={{0,9},{1,8},{2,11},{3,10},{4,13},{5,12},{6,15},{7,14},{8,1},{9,0},... | collective-permute-start | bytes 12296 | tf_op jit(solution)/shard_map/ppermute | solution.py:309
  15.1 1.2 %collective-permute-start.3 = (s32[8,1,256]{2,1,0:T(1,128)S(1)}, s32[8,1,256]{2,1,0:T(1,128)S(1)}, u32[]{:S(2)}, u32[]{:S(2)}) collective-permute-start(s32[8,1,256]{2,1,0:T(1,128)S(1)} %pad_add_fusion), channel_id=1, source_target_pairs={{0,1},{1,0},{2,3},{3,2},{4,5},{5,4},{6,7},{7,6},{8,9},{9,8},{10,11... | collective-permute-start | bytes 24584 | tf_op jit(solution)/shard_map/ppermute | solution.py:309
where the time goes:
time: 24.9 us; the launch traced here: 24.6 us
  Pallas kernels  12.9 us (52%)
  starting transfers between devices  7.48 us (30%)
  waiting for transfers between devices  3.44 us (14%)
  local copies, waits for them, and re-layouts  0.75 us (3%)
    pallas_call x1, Pallas kernels, probe_call(): pl.pallas_call(probe_kernel, out_shape=jax.ShapeDtypeStruct((CAP, WINDOW,...  8.26 us
    ppermute x4, starting transfers between devices, local(): other = lax.ppermute(every, 'beam', pairs)  7.48 us
    ppermute x4, waiting for transfers between devices, local(): other = lax.ppermute(every, 'beam', pairs)  3.44 us
    pallas_call x1, Pallas kernels, local(): pl.pallas_call(pick_kernel, out_shape=(pltpu.VMEM((CAP, 2, beam_total, 12...  1.85 us
    pallas_call x1, Pallas kernels, local(): pl.pallas_call(place_kernel, out_shape=pltpu.VMEM((CAP, 2, length, 2 * WI...  1.56 us
    pallas_call x1, Pallas kernels, local(): pl.pallas_call(fetch_kernel, out_shape=pltpu.VMEM((2, length, length // 2...  1.23 us
    broadcast_in_dim x1, local copies, waits for them, and re-layouts, local(): every = jnp.broadcast_to(beams[:, :, None], (1, 2, 128)).reshape(1, 1, 256)  0.72 us
  transfers between devices with their start and end apart: 4, of which 3 were waited for; matrix products, arithmetic and copies ran while one was open for 0% of the time, Pallas kernels for 19%

commit v1 on v0

--- a/solution.py
+++ b/solution.py
@@ -65,15 +65,52 @@
     return jnp.where(inside, rows[:-1], rows[1:]).reshape(length, width)
 
 
-def pick_kernel(owner_hbm, position_hbm, phase_hbm, weight_ref, offset_ref, owner_ref, position_ref, phase_ref, pick_ref, sems):
-    slots, (beams, probes) = weight_ref.shape[0], phase_ref.shape
-    pairs = [(owner_hbm, owner_ref), (position_hbm, position_ref), (phase_hbm, phase_ref)]
+def pick_kernel(owner_hbm, position_hbm, pick_ref, owner_ref, position_ref, slot_ref, sems):
+    slots, probes = pick_ref.shape[0] // 3, owner_ref.shape[0]
+    pairs = [(owner_hbm, owner_ref), (position_hbm, position_ref)]
     copies = [pltpu.make_async_copy(*pair, sems.at[index]) for index, pair in enumerate(pairs)]
     for copy in copies:
         copy.start()
     me = lax.axis_index("beam")
     for slot in range(slots):
-        pick_ref[slot] = -1
+        slot_ref[slot] = -1
+    copies[0].wait()
+
+    def visit(probe, count):
+        hit = owner_ref[probe] == me
+        slot_ref[jnp.where(hit, count, slots)] = probe
+        return count + jnp.where(hit, 1, 0)
+
+    lax.fori_loop(0, probes, visit, 0, unroll=math.gcd(probes, 32))
+    copies[1].wait()
+    for slot in range(slots):
+        probe = jnp.maximum(slot_ref[slot], 0)
+        pick_ref[3 * slot] = slot_ref[slot]
+        pick_ref[3 * slot + 1] = position_ref[0, probe]
+        pick_ref[3 * slot + 2] = position_ref[1, probe]
+
+
+def fetch_kernel(specimen_hbm, specimen_ref, sem):
+    copy = pltpu.make_async_copy(specimen_hbm.at[0, :, :, 0 : specimen_ref.shape[2]], specimen_ref, sem)
+    copy.start()
+    copy.wait()
+
+
+def place_kernel(pick_hbm, phase_hbm, table_hbm, weight_ref, right_ref, pick_ref, phase_ref, table_ref, sems):
+    slots, length = right_ref.shape[0], right_ref.shape[2]
+    beams, probes = phase_ref.shape
+    half = length // 2
+    cut = half + SPAN + 8
+    pairs = [
+        (pick_hbm, pick_ref),
+        (phase_hbm, phase_ref),
+        (table_hbm.at[0:cut], table_ref.at[0:cut]),
+        (table_hbm.at[cut:], table_ref.at[cut:]),
+    ]
+    copies = [pltpu.make_async_copy(*pair, sems.at[index]) for index, pair in enumerate(pairs)]
+    for copy in copies:
+        copy.start()
+    me = lax.axis_index("beam")
     lane = lax.broadcasted_iota(jnp.int32, (beams, probes), 1)
     row = lax.broadcasted_iota(jnp.int32, (beams, 128), 0)
     column = lax.broadcasted_iota(jnp.int32, (beams, 128), 1)
@@ -81,17 +118,9 @@
     for step, mask in enumerate(partners(beams)):
         flips = flips ^ jnp.where((column >> step & 1) == 1, mask, 0)
     copies[0].wait()
-
-    def visit(probe, count):
-        hit = owner_ref[probe] == me
-        pick_ref[jnp.where(hit, count, slots)] = probe
-        return count + jnp.where(hit, 1, 0)
-
-    lax.fori_loop(0, probes, visit, 0)
-    for copy in copies[1:]:
-        copy.wait()
-    for slot in range(slots):
-        pick = pick_ref[slot]
+    copies[1].wait()
+    for slot in range(slots):
+        pick = pick_ref[3 * slot]
         level = jnp.sum(jnp.where(lane == pick, phase_ref[...], 0), axis=1, keepdims=True)
         level = jnp.sum(jnp.where(row == flips ^ me, level, 0), axis=0, keepdims=True)
         level = jnp.sum(jnp.where(row == column, level, 0), axis=1, keepdims=True)
@@ -99,30 +128,12 @@
         scale = jnp.where(pick >= 0, 1.0 / math.sqrt(beams), 0.0)
         weight_ref[slot, 0] = cosine(level, LEVELS) * scale
         weight_ref[slot, 1] = cosine(level - LEVELS // 4, LEVELS) * scale
-        probe = jnp.maximum(pick, 0)
-        offset_ref[2 * slot] = position_ref[0, probe]
-        offset_ref[2 * slot + 1] = position_ref[1, probe]
-
-
-def fetch_kernel(specimen_hbm, specimen_ref, sem):
-    copy = pltpu.make_async_copy(specimen_hbm.at[0, :, :, 0 : specimen_ref.shape[2]], specimen_ref, sem)
-    copy.start()
-    copy.wait()
-
-
-def place_kernel(offset_hbm, table_hbm, right_ref, offset_ref, table_ref, sems):
-    slots, length = right_ref.shape[0], right_ref.shape[2]
-    copies = [
-        pltpu.make_async_copy(table_hbm, table_ref, sems.at[0]),
-        pltpu.make_async_copy(offset_hbm, offset_ref, sems.at[1]),
-    ]
-    for copy in copies:
-        copy.start()
-    for copy in copies:
-        copy.wait()
-    for slot in range(slots):
-        cols = moved(table_ref, SPAN - offset_ref[2 * slot + 1], length)
-        right_ref[slot, 0], right_ref[slot, 1] = split(cols)
+    for part in range(2):
+        copies[2 + part].wait()
+        rows = slice(part * half, (part + 1) * half)
+        for slot in range(slots):
+            cols = moved(table_ref, part * half + SPAN - pick_ref[3 * slot + 2], half)
+            right_ref[slot, 0, rows], right_ref[slot, 1, rows] = split(cols)
 
 
 def cosine(turns, length):
@@ -154,7 +165,7 @@
     mix_ref,
     light_ref,
     lit_ref,
-    half_ref,
+    half_refs,
     out_ref,
     start_ref,
     sems,
@@ -234,16 +245,15 @@
             source += [lit_ref[way, stretch, 0], lit_ref[way, stretch, 0], lit_ref[way, stretch, 1]]
             operator += [high, low, high]
         half = dot(jnp.concatenate(source, axis=1), jnp.concatenate(operator, axis=0))
-        half_ref[way, 0:length] = half
-        half_ref[way, length:] = half[0 : SPAN + 8]
+        half_refs[way][0:length] = half
+        half_refs[way][length:] = half[0 : SPAN + 8]
 
     def along_rows(slot, way):
-        high, low = split(moved(half_ref.at[way], start_ref[2 * slot], length))
+        high, low = split(moved(half_refs[way], start_ref[3 * slot + 1], length))
         full = dot(left_ref[...], jnp.concatenate([high, low, high], axis=0))
         real = full[:WINDOW, :WINDOW] - full[WINDOW:, WINDOW:]
         imag = full[:WINDOW, WINDOW:] + full[WINDOW:, :WINDOW]
         out_ref[slot] = real * real + imag * imag
-        pltpu.make_async_copy(out_ref.at[slot], out_hbm.at[slot], out_sems.at[slot]).start()
 
     def prepare(slot):
         light(slot, slot)
@@ -255,15 +265,20 @@
             shine(tile - 1, slot)
         shine(length // 128 - 1, slot)
 
+    def send(slot):
+        pltpu.make_async_copy(out_ref.at[slot], out_hbm.at[slot], out_sems.at[slot]).start()
+
     prepare(0)
     for slot in range(slots):
-        along_cols(slot, slot)
         if slot + 1 < slots:
             prepare(slot + 1)
+        along_cols(slot, slot)
     copy.wait()
     left.wait()
     for slot in range(slots):
         along_rows(slot, slot)
+    for slot in range(slots):
+        send(slot)
     for slot in range(slots):
         pltpu.make_async_copy(out_ref.at[slot], out_hbm.at[slot], out_sems.at[slot]).wait()
 
@@ -288,9 +303,9 @@
             pltpu.VMEM((CAP, depth, 2 * length), jnp.bfloat16),
             pltpu.VMEM((CAP, length // 128, length, 256), jnp.float32),
             pltpu.VMEM((CAP, 2 * length // WIDE, 2, length, WIDE), jnp.bfloat16),
-            pltpu.VMEM((CAP, length + SPAN + 8, 2 * WINDOW), jnp.float32),
+            [pltpu.VMEM((length + SPAN + 8, 2 * WINDOW), jnp.float32) for _ in range(CAP)],
             pltpu.VMEM((CAP, WINDOW, WINDOW), jnp.float32),
-            pltpu.SMEM((2 * CAP,), jnp.int32),
+            pltpu.SMEM((3 * CAP,), jnp.int32),
             pltpu.SemaphoreType.DMA((3,)),
             pltpu.SemaphoreType.DMA((CAP,)),
         ],
@@ -312,24 +327,20 @@
     smem = pl.BlockSpec(memory_space=pltpu.SMEM)
     anywhere = pl.BlockSpec(memory_space=pltpu.HBM)
     params = pltpu.CompilerParams(vmem_limit_bytes=VMEM_LIMIT)
-    weight, offset = pl.pallas_call(
+    pick = pl.pallas_call(
         pick_kernel,
-        out_shape=(
-            pltpu.VMEM((CAP, 2, beam_total, 128), jnp.float32),
-            jax.ShapeDtypeStruct((2 * CAP,), jnp.int32),
-        ),
-        in_specs=[anywhere] * 3,
-        out_specs=(vmem, smem),
+        out_shape=jax.ShapeDtypeStruct((3 * CAP,), jnp.int32),
+        in_specs=[anywhere] * 2,
+        out_specs=smem,
         scratch_shapes=[
             pltpu.SMEM(owner.shape, jnp.int32),
             pltpu.SMEM(positions.shape[::-1], jnp.int32),
-            pltpu.VMEM(phases.shape[::-1], jnp.int32),
             pltpu.SMEM((CAP + 1,), jnp.int32),
-            pltpu.SemaphoreType.DMA((3,)),
+            pltpu.SemaphoreType.DMA((2,)),
         ],
         compiler_params=params,
         name="pick",
-    )(*(pltpu.with_memory_space_constraint(x, pltpu.HBM) for x in (owner, positions.T, phases.T)))
+    )(*(pltpu.with_memory_space_constraint(x, pltpu.HBM) for x in (owner, positions.T)))
     specimen = pl.pallas_call(
         fetch_kernel,
         out_shape=pltpu.VMEM((2, length, length // 2), jnp.float32),
@@ -340,20 +351,24 @@
         name="fetch",
     )(pltpu.with_memory_space_constraint(transmission, pltpu.HBM))
     table = window_operator(length)
-    right = pl.pallas_call(
+    weight, right = pl.pallas_call(
         place_kernel,
-        out_shape=pltpu.VMEM((CAP, 2, length, 2 * WINDOW), jnp.bfloat16),
-        in_specs=[pl.BlockSpec(memory_space=pl.ANY), anywhere],
-        out_specs=vmem,
+        out_shape=(
+            pltpu.VMEM((CAP, 2, beam_total, 128), jnp.float32),
+            pltpu.VMEM((CAP, 2, length, 2 * WINDOW), jnp.bfloat16),
+        ),
+        in_specs=[pl.BlockSpec(memory_space=pl.ANY), anywhere, anywhere],
+        out_specs=(vmem, vmem),
         scratch_shapes=[
-            pltpu.SMEM((2 * CAP,), jnp.int32),
+            pltpu.SMEM((3 * CAP,), jnp.int32),
+            pltpu.VMEM(phases.shape[::-1], jnp.int32),
             pltpu.VMEM(table.shape, jnp.float32),
-            pltpu.SemaphoreType.DMA((2,)),
+            pltpu.SemaphoreType.DMA((4,)),
         ],
         compiler_params=params,
         name="place",
-    )(offset, pltpu.with_memory_space_constraint(jnp.asarray(table), pltpu.HBM))
-    return probe_call(every, weight, specimen, right, offset, transmission, jnp.asarray(row_operator(table)))
+    )(pick, *(pltpu.with_memory_space_constraint(x, pltpu.HBM) for x in (phases.T, jnp.asarray(table))))
+    return probe_call(every, weight, specimen, right, pick, transmission, jnp.asarray(row_operator(table)))
 
 
 def solution(mesh):

time: 24.9 us -> 23.9 us (0.960)
  Pallas kernels: 12.9 us -> 11.9 us
    pallas_call x2, Pallas kernels: 3.41 us -> 2.87 us  [the longest x1 1.48 us: local(): pl.pallas_call(place_kernel, out_shape=(pltpu.VMEM((CAP, 2, beam_total, 1...]
    pallas_call x1, Pallas kernels: 8.26 us -> 7.84 us  [probe_call(): pl.pallas_call(probe_kernel, out_shape=jax.ShapeDtypeStruct((CAP, WINDOW,...]
  transfers between devices with their start and end apart: 4 -> 4, of which waited for: 3 -> 3; matrix products, arithmetic and copies ran while one was open for 0% -> 0% of each run, Pallas kernels for 19% -> 17%
where the time goes in v1:
time: 23.9 us; the launch traced here: 23.7 us
  Pallas kernels  11.9 us (50%)
  starting transfers between devices  7.48 us (31%)
  waiting for transfers between devices  3.44 us (14%)
  local copies, waits for them, and re-layouts  0.75 us (3%)
    pallas_call x1, Pallas kernels, probe_call(): pl.pallas_call(probe_kernel, out_shape=jax.ShapeDtypeStruct((CAP, WINDOW,...  7.84 us
    ppermute x4, starting transfers between devices, local(): other = lax.ppermute(every, 'beam', pairs)  7.48 us
    ppermute x4, waiting for transfers between devices, local(): other = lax.ppermute(every, 'beam', pairs)  3.44 us
    pallas_call x1, Pallas kernels, local(): pl.pallas_call(place_kernel, out_shape=(pltpu.VMEM((CAP, 2, beam_total, 1...  1.48 us
    pallas_call x1, Pallas kernels, local(): pl.pallas_call(pick_kernel, out_shape=jax.ShapeDtypeStruct((3 * CAP,), jn...  1.39 us
    pallas_call x1, Pallas kernels, local(): pl.pallas_call(fetch_kernel, out_shape=pltpu.VMEM((2, length, length // 2...  1.23 us
    broadcast_in_dim x1, local copies, waits for them, and re-layouts, local(): every = jnp.broadcast_to(beams[:, :, None], (1, 2, 128)).reshape(1, 1, 256)  0.72 us
  transfers between devices with their start and end apart: 4, of which 3 were waited for; matrix products, arithmetic and copies ran while one was open for 0% of the time, Pallas kernels for 17%

profile of v1, /device:TPU:0, one launch (start us, length us, event | category | flops | bytes accessed | tf_op | source)
XLA Modules:
  0.0 23.7 jit_solution(3088540931738242381)
XLA Ops:
  0.0 0.7 %broadcast_in_dim.11 = s32[2,128]{1,0:T(2,128)S(1)} broadcast(s32[2]{0:T(128)} %bitcast.11), dimensions={0} | broadcast | bytes 1032 | tf_op jit(solution)/shard_map/broadcast_in_dim | solution.py:321
  0.7 2.4 %collective-permute-start = (s32[1,1,256]{2,1,0:T(1,128)S(1)}, s32[1,1,256]{2,1,0:T(1,128)S(1)}, u32[]{:S(2)}, u32[]{:S(2)}) collective-permute-start(s32[1,1,256]{2,1,0:T(1,128)S(1)} %bitcast.4), channel_id=1, source_target_pairs={{0,3},{1,2},{2,1},{3,0},{4,7},{5,6},{6,5},{7,4},{8,11},{9,10},{10,... | collective-permute-start | bytes 3080 | tf_op jit(solution)/shard_map/ppermute | solution.py:324
  3.2 1.2 %fetch.1.near_ref = f32[2,512,256]{2,1,0:T(8,128)S(1)} custom-call(f32[1,2,512,512]{3,2,1,0:T(8,128)} %transmission_hbm.1), custom_call_target="tpu_custom_call" | custom-call | tf_op jit(solution)/shard_map/fetch/pallas_call | solution.py:344
  4.4 1.4 %pick.1.pick_hbm.offset_ref = s32[12]{0:T(128)S(1)} custom-call(s32[32]{0:T(128)} %owner_hbm.1, s32[2,32]{1,0:T(2,128)} %bitcast.10), custom_call_target="tpu_custom_call" | custom-call | tf_op jit(solution)/shard_map/pick/pallas_call | solution.py:330
  5.8 1.5 %place.1 = (f32[4,2,16,128]{3,2,1,0:T(8,128)S(1)}, bf16[4,2,512,256]{3,2,1,0:T(8,128)(2,1)S(1)}) custom-call(s32[12]{0:T(128)S(1)} %pick.1.pick_hbm.offset_ref, s32[16,32]{1,0:T(8,128)} %bitcast.9, f32[648,256]{1,0:T(8,128)} %constant.4.clone.table_hbm), custom_call_target="tpu_custom_call" | custom-call | tf_op jit(solution)/shard_map/place/pallas_call | solution.py:354
  7.3 0.0 collective-permute-done
  7.3 1.9 %collective-permute-start.1 = (s32[2,1,256]{2,1,0:T(1,128)S(1)}, s32[2,1,256]{2,1,0:T(1,128)S(1)}, u32[]{:S(2)}, u32[]{:S(2)}) collective-permute-start(s32[2,1,256]{2,1,0:T(1,128)S(1)} %pad_add_fusion.2), channel_id=1, source_target_pairs={{0,5},{1,4},{2,7},{3,6},{4,1},{5,0},{6,3},{7,2},{8,13},{9,12},{10,... | collective-permute-start | bytes 6152 | tf_op jit(solution)/shard_map/ppermute | solution.py:324
  9.2 1.3 %collective-permute-done.1 = s32[2,1,256]{2,1,0:T(1,128)S(1)} collective-permute-done((s32[2,1,256]{2,1,0:T(1,128)S(1)}, s32[2,1,256]{2,1,0:T(1,128)S(1)}, u32[]{:S(2)}, u32[]{:S(2)}) %collective-permute-start.1) | collective-permute-done | bytes 2080 | tf_op jit(solution)/shard_map/ppermute | solution.py:324
  10.5 2.7 %collective-permute-start.2 = (s32[4,1,256]{2,1,0:T(1,128)S(1)}, s32[4,1,256]{2,1,0:T(1,128)S(1)}, u32[]{:S(2)}, u32[]{:S(2)}) collective-permute-start(s32[4,1,256]{2,1,0:T(1,128)S(1)} %pad_add_fusion.1), channel_id=1, source_target_pairs={{0,9},{1,8},{2,11},{3,10},{4,13},{5,12},{6,15},{7,14},{8,1},{9,0},... | collective-permute-start | bytes 12296 | tf_op jit(solution)/shard_map/ppermute | solution.py:324
  13.3 1.3 %collective-permute-done.2 = s32[4,1,256]{2,1,0:T(1,128)S(1)} collective-permute-done((s32[4,1,256]{2,1,0:T(1,128)S(1)}, s32[4,1,256]{2,1,0:T(1,128)S(1)}, u32[]{:S(2)}, u32[]{:S(2)}) %collective-permute-start.2) | collective-permute-done | bytes 4128 | tf_op jit(solution)/shard_map/ppermute | solution.py:324
  14.6 0.4 %collective-permute-start.3 = (s32[8,1,256]{2,1,0:T(1,128)S(1)}, s32[8,1,256]{2,1,0:T(1,128)S(1)}, u32[]{:S(2)}, u32[]{:S(2)}) collective-permute-start(s32[8,1,256]{2,1,0:T(1,128)S(1)} %pad_add_fusion), channel_id=1, source_target_pairs={{0,1},{1,0},{2,3},{3,2},{4,5},{5,4},{6,7},{7,6},{8,9},{9,8},{10,11... | collective-permute-start | bytes 24584 | tf_op jit(solution)/shard_map/ppermute | solution.py:324
  15.0 0.8 %collective-permute-done.3 = s32[8,1,256]{2,1,0:T(1,128)S(1)} collective-permute-done((s32[8,1,256]{2,1,0:T(1,128)S(1)}, s32[8,1,256]{2,1,0:T(1,128)S(1)}, u32[]{:S(2)}, u32[]{:S(2)}) %collective-permute-start.3) | collective-permute-done | bytes 8224 | tf_op jit(solution)/shard_map/ppermute | solution.py:324
  15.8 7.8 %probes.1 = f32[4,128,128]{2,1,0:T(8,128)} custom-call(s32[16,1,256]{2,1,0:T(1,128)S(1)} %constant_dynamic-update-slice_fusion.beam_ref, f32[4,2,16,128]{3,2,1,0:T(8,128)S(1)} %get-tuple-element.7.weight_ref, f32[2,512,256]{2,1,0:T(8,128)S(1)} %fetch.1.near_ref, bf16[4,2,512,256]{3,2,1,0:T(8,128)(2,1)S(1)} %get-tuple-element.8.right_ref, ...), custom_call_target="tpu_custom_call" | custom-call | tf_op jit(solution)/shard_map/probes/pallas_call | solution.py:293
  (8 shorter events, 0.0 us)
Async XLA Ops:
  0.7 6.6 %collective-permute-start = (s32[1,1,256]{2,1,0:T(1,128)S(1)}, s32[1,1,256]{2,1,0:T(1,128)S(1)}, u32[]{:S(2)}, u32[]{:S(2)}) collective-permute-start(s32[1,1,256]{2,1,0:T(1,128)S(1)} %bitcast.4), channel_id=1, source_target_pairs={{0,3},{1,2},{2,1},{3,0},{4,7},{5,6},{6,5},{7,4},{8,11},{9,10},{10,... | collective-permute-start | bytes 3080 | tf_op jit(solution)/shard_map/ppermute | solution.py:324
  7.3 3.2 %collective-permute-start.1 = (s32[2,1,256]{2,1,0:T(1,128)S(1)}, s32[2,1,256]{2,1,0:T(1,128)S(1)}, u32[]{:S(2)}, u32[]{:S(2)}) collective-permute-start(s32[2,1,256]{2,1,0:T(1,128)S(1)} %pad_add_fusion.2), channel_id=1, source_target_pairs={{0,5},{1,4},{2,7},{3,6},{4,1},{5,0},{6,3},{7,2},{8,13},{9,12},{10,... | collective-permute-start | bytes 6152 | tf_op jit(solution)/shard_map/ppermute | solution.py:324
  10.5 4.0 %collective-permute-start.2 = (s32[4,1,256]{2,1,0:T(1,128)S(1)}, s32[4,1,256]{2,1,0:T(1,128)S(1)}, u32[]{:S(2)}, u32[]{:S(2)}) collective-permute-start(s32[4,1,256]{2,1,0:T(1,128)S(1)} %pad_add_fusion.1), channel_id=1, source_target_pairs={{0,9},{1,8},{2,11},{3,10},{4,13},{5,12},{6,15},{7,14},{8,1},{9,0},... | collective-permute-start | bytes 12296 | tf_op jit(solution)/shard_map/ppermute | solution.py:324
  14.6 1.2 %collective-permute-start.3 = (s32[8,1,256]{2,1,0:T(1,128)S(1)}, s32[8,1,256]{2,1,0:T(1,128)S(1)}, u32[]{:S(2)}, u32[]{:S(2)}) collective-permute-start(s32[8,1,256]{2,1,0:T(1,128)S(1)} %pad_add_fusion), channel_id=1, source_target_pairs={{0,1},{1,0},{2,3},{3,2},{4,5},{5,4},{6,7},{7,6},{8,9},{9,8},{10,11... | collective-permute-start | bytes 24584 | tf_op jit(solution)/shard_map/ppermute | solution.py:324

commit v2 on v1

--- a/solution.py
+++ b/solution.py
@@ -43,7 +43,7 @@
 
 
 def partners(count):
-    return [1 << bit | 1 for bit in range(1, count.bit_length() - 1)] + [1]
+    return [1 << bit | 1 for bit in range(count.bit_length() - 2, 0, -1)] + [1]
 
 
 def split(value):
@@ -268,15 +268,24 @@
     def send(slot):
         pltpu.make_async_copy(out_ref.at[slot], out_hbm.at[slot], out_sems.at[slot]).start()
 
-    prepare(0)
-    for slot in range(slots):
-        if slot + 1 < slots:
-            prepare(slot + 1)
-        along_cols(slot, slot)
+    def run(count):
+        ready = 0
+        for slot in range(count):
+            wanted = min(slot + 2 if count == slots or slot else 1, count)
+            for coming in range(ready, wanted):
+                prepare(coming)
+            ready = wanted
+            along_cols(slot, slot)
+        left.wait()
+        for slot in range(count):
+            along_rows(slot, slot)
+        for slot in range(count, slots):
+            out_ref[slot] = jnp.zeros((WINDOW, WINDOW), jnp.float32)
+
     copy.wait()
-    left.wait()
-    for slot in range(slots):
-        along_rows(slot, slot)
+    full = start_ref[3 * slots - 3] >= 0
+    pl.when(full)(lambda: run(slots))
+    pl.when(jnp.logical_not(full))(lambda: run(slots - 1))
     for slot in range(slots):
         send(slot)
     for slot in range(slots):

time: 23.9 us -> 22.9 us (0.958)
  Pallas kernels: 11.9 us -> 10.8 us
    pallas_call x1, Pallas kernels: 7.84 us -> 6.71 us  [probe_call(): pl.pallas_call(probe_kernel, out_shape=jax.ShapeDtypeStruct((CAP, WINDOW,...]
  transfers between devices with their start and end apart: 4 -> 4, of which waited for: 3 -> 3; matrix products, arithmetic and copies ran while one was open for 0% -> 0% of each run, Pallas kernels for 17% -> 18%
where the time goes in v2:
time: 22.9 us; the launch traced here: 22.7 us
  Pallas kernels  10.8 us (47%)
  starting transfers between devices  7.59 us (33%)
  waiting for transfers between devices  3.5 us (15%)
  local copies, waits for them, and re-layouts  0.75 us (3%)
    ppermute x4, starting transfers between devices, local(): other = lax.ppermute(every, 'beam', pairs)  7.59 us
    pallas_call x1, Pallas kernels, probe_call(): pl.pallas_call(probe_kernel, out_shape=jax.ShapeDtypeStruct((CAP, WINDOW,...  6.71 us
    ppermute x4, waiting for transfers between devices, local(): other = lax.ppermute(every, 'beam', pairs)  3.5 us
    pallas_call x1, Pallas kernels, local(): pl.pallas_call(place_kernel, out_shape=(pltpu.VMEM((CAP, 2, beam_total, 1...  1.48 us
    pallas_call x1, Pallas kernels, local(): pl.pallas_call(pick_kernel, out_shape=jax.ShapeDtypeStruct((3 * CAP,), jn...  1.39 us
    pallas_call x1, Pallas kernels, local(): pl.pallas_call(fetch_kernel, out_shape=pltpu.VMEM((2, length, length // 2...  1.23 us
    broadcast_in_dim x1, local copies, waits for them, and re-layouts, local(): every = jnp.broadcast_to(beams[:, :, None], (1, 2, 128)).reshape(1, 1, 256)  0.72 us
  transfers between devices with their start and end apart: 4, of which 3 were waited for; matrix products, arithmetic and copies ran while one was open for 0% of the time, Pallas kernels for 18%

profile of v2, /device:TPU:0, one launch (start us, length us, event | category | flops | bytes accessed | tf_op | source)
XLA Modules:
  0.0 22.7 jit_solution(6579785793052966179)
XLA Ops:
  0.0 0.7 %broadcast_in_dim.11 = s32[2,128]{1,0:T(2,128)S(1)} broadcast(s32[2]{0:T(128)} %bitcast.11), dimensions={0} | broadcast | bytes 1032 | tf_op jit(solution)/shard_map/broadcast_in_dim | solution.py:330
  0.7 3.5 %collective-permute-start = (s32[1,1,256]{2,1,0:T(1,128)S(1)}, s32[1,1,256]{2,1,0:T(1,128)S(1)}, u32[]{:S(2)}, u32[]{:S(2)}) collective-permute-start(s32[1,1,256]{2,1,0:T(1,128)S(1)} %bitcast.4), channel_id=1, source_target_pairs={{0,9},{1,8},{2,11},{3,10},{4,13},{5,12},{6,15},{7,14},{8,1},{9,0},... | collective-permute-start | bytes 3080 | tf_op jit(solution)/shard_map/ppermute | solution.py:333
  4.2 1.2 %fetch.1.near_ref = f32[2,512,256]{2,1,0:T(8,128)S(1)} custom-call(f32[1,2,512,512]{3,2,1,0:T(8,128)} %transmission_hbm.1), custom_call_target="tpu_custom_call" | custom-call | tf_op jit(solution)/shard_map/fetch/pallas_call | solution.py:353
  5.5 1.4 %pick.1.pick_hbm.offset_ref = s32[12]{0:T(128)S(1)} custom-call(s32[32]{0:T(128)} %owner_hbm.1, s32[2,32]{1,0:T(2,128)} %bitcast.10), custom_call_target="tpu_custom_call" | custom-call | tf_op jit(solution)/shard_map/pick/pallas_call | solution.py:339
  6.9 1.5 %place.1 = (f32[4,2,16,128]{3,2,1,0:T(8,128)S(1)}, bf16[4,2,512,256]{3,2,1,0:T(8,128)(2,1)S(1)}) custom-call(s32[12]{0:T(128)S(1)} %pick.1.pick_hbm.offset_ref, s32[16,32]{1,0:T(8,128)} %bitcast.9, f32[648,256]{1,0:T(8,128)} %constant.4.clone.table_hbm), custom_call_target="tpu_custom_call" | custom-call | tf_op jit(solution)/shard_map/place/pallas_call | solution.py:363
  8.4 0.0 collective-permute-done
  8.4 1.9 %collective-permute-start.1 = (s32[2,1,256]{2,1,0:T(1,128)S(1)}, s32[2,1,256]{2,1,0:T(1,128)S(1)}, u32[]{:S(2)}, u32[]{:S(2)}) collective-permute-start(s32[2,1,256]{2,1,0:T(1,128)S(1)} %pad_add_fusion.2), channel_id=1, source_target_pairs={{0,5},{1,4},{2,7},{3,6},{4,1},{5,0},{6,3},{7,2},{8,13},{9,12},{10,... | collective-permute-start | bytes 6152 | tf_op jit(solution)/shard_map/ppermute | solution.py:333
  10.3 1.3 %collective-permute-done.1 = s32[2,1,256]{2,1,0:T(1,128)S(1)} collective-permute-done((s32[2,1,256]{2,1,0:T(1,128)S(1)}, s32[2,1,256]{2,1,0:T(1,128)S(1)}, u32[]{:S(2)}, u32[]{:S(2)}) %collective-permute-start.1) | collective-permute-done | bytes 2080 | tf_op jit(solution)/shard_map/ppermute | solution.py:333
  11.6 1.6 %collective-permute-start.2 = (s32[4,1,256]{2,1,0:T(1,128)S(1)}, s32[4,1,256]{2,1,0:T(1,128)S(1)}, u32[]{:S(2)}, u32[]{:S(2)}) collective-permute-start(s32[4,1,256]{2,1,0:T(1,128)S(1)} %pad_add_fusion.1), channel_id=1, source_target_pairs={{0,3},{1,2},{2,1},{3,0},{4,7},{5,6},{6,5},{7,4},{8,11},{9,10},{10,... | collective-permute-start | bytes 12296 | tf_op jit(solution)/shard_map/ppermute | solution.py:333
  13.3 1.4 %collective-permute-done.2 = s32[4,1,256]{2,1,0:T(1,128)S(1)} collective-permute-done((s32[4,1,256]{2,1,0:T(1,128)S(1)}, s32[4,1,256]{2,1,0:T(1,128)S(1)}, u32[]{:S(2)}, u32[]{:S(2)}) %collective-permute-start.2) | collective-permute-done | bytes 4128 | tf_op jit(solution)/shard_map/ppermute | solution.py:333
  14.6 0.5 %collective-permute-start.3 = (s32[8,1,256]{2,1,0:T(1,128)S(1)}, s32[8,1,256]{2,1,0:T(1,128)S(1)}, u32[]{:S(2)}, u32[]{:S(2)}) collective-permute-start(s32[8,1,256]{2,1,0:T(1,128)S(1)} %pad_add_fusion), channel_id=1, source_target_pairs={{0,1},{1,0},{2,3},{3,2},{4,5},{5,4},{6,7},{7,6},{8,9},{9,8},{10,11... | collective-permute-start | bytes 24584 | tf_op jit(solution)/shard_map/ppermute | solution.py:333
  15.2 0.8 %collective-permute-done.3 = s32[8,1,256]{2,1,0:T(1,128)S(1)} collective-permute-done((s32[8,1,256]{2,1,0:T(1,128)S(1)}, s32[8,1,256]{2,1,0:T(1,128)S(1)}, u32[]{:S(2)}, u32[]{:S(2)}) %collective-permute-start.3) | collective-permute-done | bytes 8224 | tf_op jit(solution)/shard_map/ppermute | solution.py:333
  16.0 6.7 %probes.1 = f32[4,128,128]{2,1,0:T(8,128)} custom-call(s32[16,1,256]{2,1,0:T(1,128)S(1)} %constant_dynamic-update-slice_fusion.beam_ref, f32[4,2,16,128]{3,2,1,0:T(8,128)S(1)} %get-tuple-element.7.weight_ref, f32[2,512,256]{2,1,0:T(8,128)S(1)} %fetch.1.near_ref, bf16[4,2,512,256]{3,2,1,0:T(8,128)(2,1)S(1)} %get-tuple-element.8.right_ref, ...), custom_call_target="tpu_custom_call" | custom-call | tf_op jit(solution)/shard_map/probes/pallas_call | solution.py:302
  (8 shorter events, 0.0 us)
Async XLA Ops:
  0.7 7.6 %collective-permute-start = (s32[1,1,256]{2,1,0:T(1,128)S(1)}, s32[1,1,256]{2,1,0:T(1,128)S(1)}, u32[]{:S(2)}, u32[]{:S(2)}) collective-permute-start(s32[1,1,256]{2,1,0:T(1,128)S(1)} %bitcast.4), channel_id=1, source_target_pairs={{0,9},{1,8},{2,11},{3,10},{4,13},{5,12},{6,15},{7,14},{8,1},{9,0},... | collective-permute-start | bytes 3080 | tf_op jit(solution)/shard_map/ppermute | solution.py:333
  8.4 3.2 %collective-permute-start.1 = (s32[2,1,256]{2,1,0:T(1,128)S(1)}, s32[2,1,256]{2,1,0:T(1,128)S(1)}, u32[]{:S(2)}, u32[]{:S(2)}) collective-permute-start(s32[2,1,256]{2,1,0:T(1,128)S(1)} %pad_add_fusion.2), channel_id=1, source_target_pairs={{0,5},{1,4},{2,7},{3,6},{4,1},{5,0},{6,3},{7,2},{8,13},{9,12},{10,... | collective-permute-start | bytes 6152 | tf_op jit(solution)/shard_map/ppermute | solution.py:333
  11.6 3.0 %collective-permute-start.2 = (s32[4,1,256]{2,1,0:T(1,128)S(1)}, s32[4,1,256]{2,1,0:T(1,128)S(1)}, u32[]{:S(2)}, u32[]{:S(2)}) collective-permute-start(s32[4,1,256]{2,1,0:T(1,128)S(1)} %pad_add_fusion.1), channel_id=1, source_target_pairs={{0,3},{1,2},{2,1},{3,0},{4,7},{5,6},{6,5},{7,4},{8,11},{9,10},{10,... | collective-permute-start | bytes 12296 | tf_op jit(solution)/shard_map/ppermute | solution.py:333
  14.6 1.3 %collective-permute-start.3 = (s32[8,1,256]{2,1,0:T(1,128)S(1)}, s32[8,1,256]{2,1,0:T(1,128)S(1)}, u32[]{:S(2)}, u32[]{:S(2)}) collective-permute-start(s32[8,1,256]{2,1,0:T(1,128)S(1)} %pad_add_fusion), channel_id=1, source_target_pairs={{0,1},{1,0},{2,3},{3,2},{4,5},{5,4},{6,7},{7,6},{8,9},{9,8},{10,11... | collective-permute-start | bytes 24584 | tf_op jit(solution)/shard_map/ppermute | solution.py:333

commit v3 on v2

--- a/solution.py
+++ b/solution.py
@@ -248,12 +248,17 @@
         half_refs[way][0:length] = half
         half_refs[way][length:] = half[0 : SPAN + 8]
 
-    def along_rows(slot, way):
-        high, low = split(moved(half_refs[way], start_ref[3 * slot + 1], length))
-        full = dot(left_ref[...], jnp.concatenate([high, low, high], axis=0))
-        real = full[:WINDOW, :WINDOW] - full[WINDOW:, WINDOW:]
-        imag = full[:WINDOW, WINDOW:] + full[WINDOW:, :WINDOW]
-        out_ref[slot] = real * real + imag * imag
+    def along_rows(count):
+        parts = []
+        for slot in range(count):
+            high, low = split(moved(half_refs[slot], start_ref[3 * slot + 1], length))
+            parts.append(jnp.concatenate([high, low, high], axis=0))
+        every = dot(left_ref[...], jnp.concatenate(parts, axis=1))
+        for slot in range(count):
+            full = every[:, 2 * slot * WINDOW : 2 * (slot + 1) * WINDOW]
+            real = full[:WINDOW, :WINDOW] - full[WINDOW:, WINDOW:]
+            imag = full[:WINDOW, WINDOW:] + full[WINDOW:, :WINDOW]
+            out_ref[slot] = real * real + imag * imag
 
     def prepare(slot):
         light(slot, slot)
@@ -277,8 +282,7 @@
             ready = wanted
             along_cols(slot, slot)
         left.wait()
-        for slot in range(count):
-            along_rows(slot, slot)
+        along_rows(count)
         for slot in range(count, slots):
             out_ref[slot] = jnp.zeros((WINDOW, WINDOW), jnp.float32)
 

time: 22.9 us -> 22.9 us (level)
  no operation moved by 1% of the time
where the time goes in v3:
time: 22.9 us; the launch traced here: 22.7 us
  Pallas kernels  10.8 us (47%)
  starting transfers between devices  7.59 us (33%)
  waiting for transfers between devices  3.5 us (15%)
  local copies, waits for them, and re-layouts  0.75 us (3%)
    ppermute x4, starting transfers between devices, local(): other = lax.ppermute(every, 'beam', pairs)  7.59 us
    pallas_call x1, Pallas kernels, probe_call(): pl.pallas_call(probe_kernel, out_shape=jax.ShapeDtypeStruct((CAP, WINDOW,...  6.71 us
    ppermute x4, waiting for transfers between devices, local(): other = lax.ppermute(every, 'beam', pairs)  3.5 us
    pallas_call x1, Pallas kernels, local(): pl.pallas_call(place_kernel, out_shape=(pltpu.VMEM((CAP, 2, beam_total, 1...  1.48 us
    pallas_call x1, Pallas kernels, local(): pl.pallas_call(pick_kernel, out_shape=jax.ShapeDtypeStruct((3 * CAP,), jn...  1.39 us
    pallas_call x1, Pallas kernels, local(): pl.pallas_call(fetch_kernel, out_shape=pltpu.VMEM((2, length, length // 2...  1.23 us
    broadcast_in_dim x1, local copies, waits for them, and re-layouts, local(): every = jnp.broadcast_to(beams[:, :, None], (1, 2, 128)).reshape(1, 1, 256)  0.72 us
  transfers between devices with their start and end apart: 4, of which 3 were waited for; matrix products, arithmetic and copies ran while one was open for 0% of the time, Pallas kernels for 18%

profile of v3, /device:TPU:0, one launch (start us, length us, event | category | flops | bytes accessed | tf_op | source)
XLA Modules:
  0.0 22.7 jit_solution(11677145800458200864)
XLA Ops:
  0.0 0.7 %broadcast_in_dim.11 = s32[2,128]{1,0:T(2,128)S(1)} broadcast(s32[2]{0:T(128)} %bitcast.11), dimensions={0} | broadcast | bytes 1032 | tf_op jit(solution)/shard_map/broadcast_in_dim | solution.py:334
  0.7 3.5 %collective-permute-start = (s32[1,1,256]{2,1,0:T(1,128)S(1)}, s32[1,1,256]{2,1,0:T(1,128)S(1)}, u32[]{:S(2)}, u32[]{:S(2)}) collective-permute-start(s32[1,1,256]{2,1,0:T(1,128)S(1)} %bitcast.4), channel_id=1, source_target_pairs={{0,9},{1,8},{2,11},{3,10},{4,13},{5,12},{6,15},{7,14},{8,1},{9,0},... | collective-permute-start | bytes 3080 | tf_op jit(solution)/shard_map/ppermute | solution.py:337
  4.2 1.2 %fetch.1.near_ref = f32[2,512,256]{2,1,0:T(8,128)S(1)} custom-call(f32[1,2,512,512]{3,2,1,0:T(8,128)} %transmission_hbm.1), custom_call_target="tpu_custom_call" | custom-call | tf_op jit(solution)/shard_map/fetch/pallas_call | solution.py:357
  5.5 1.4 %pick.1.pick_hbm.offset_ref = s32[12]{0:T(128)S(1)} custom-call(s32[32]{0:T(128)} %owner_hbm.1, s32[2,32]{1,0:T(2,128)} %bitcast.10), custom_call_target="tpu_custom_call" | custom-call | tf_op jit(solution)/shard_map/pick/pallas_call | solution.py:343
  6.9 1.5 %place.1 = (f32[4,2,16,128]{3,2,1,0:T(8,128)S(1)}, bf16[4,2,512,256]{3,2,1,0:T(8,128)(2,1)S(1)}) custom-call(s32[12]{0:T(128)S(1)} %pick.1.pick_hbm.offset_ref, s32[16,32]{1,0:T(8,128)} %bitcast.9, f32[648,256]{1,0:T(8,128)} %constant.4.clone.table_hbm), custom_call_target="tpu_custom_call" | custom-call | tf_op jit(solution)/shard_map/place/pallas_call | solution.py:367
  8.4 0.0 collective-permute-done
  8.4 1.9 %collective-permute-start.1 = (s32[2,1,256]{2,1,0:T(1,128)S(1)}, s32[2,1,256]{2,1,0:T(1,128)S(1)}, u32[]{:S(2)}, u32[]{:S(2)}) collective-permute-start(s32[2,1,256]{2,1,0:T(1,128)S(1)} %pad_add_fusion.2), channel_id=1, source_target_pairs={{0,5},{1,4},{2,7},{3,6},{4,1},{5,0},{6,3},{7,2},{8,13},{9,12},{10,... | collective-permute-start | bytes 6152 | tf_op jit(solution)/shard_map/ppermute | solution.py:337
  10.3 1.3 %collective-permute-done.1 = s32[2,1,256]{2,1,0:T(1,128)S(1)} collective-permute-done((s32[2,1,256]{2,1,0:T(1,128)S(1)}, s32[2,1,256]{2,1,0:T(1,128)S(1)}, u32[]{:S(2)}, u32[]{:S(2)}) %collective-permute-start.1) | collective-permute-done | bytes 2080 | tf_op jit(solution)/shard_map/ppermute | solution.py:337
  11.6 1.6 %collective-permute-start.2 = (s32[4,1,256]{2,1,0:T(1,128)S(1)}, s32[4,1,256]{2,1,0:T(1,128)S(1)}, u32[]{:S(2)}, u32[]{:S(2)}) collective-permute-start(s32[4,1,256]{2,1,0:T(1,128)S(1)} %pad_add_fusion.1), channel_id=1, source_target_pairs={{0,3},{1,2},{2,1},{3,0},{4,7},{5,6},{6,5},{7,4},{8,11},{9,10},{10,... | collective-permute-start | bytes 12296 | tf_op jit(solution)/shard_map/ppermute | solution.py:337
  13.3 1.4 %collective-permute-done.2 = s32[4,1,256]{2,1,0:T(1,128)S(1)} collective-permute-done((s32[4,1,256]{2,1,0:T(1,128)S(1)}, s32[4,1,256]{2,1,0:T(1,128)S(1)}, u32[]{:S(2)}, u32[]{:S(2)}) %collective-permute-start.2) | collective-permute-done | bytes 4128 | tf_op jit(solution)/shard_map/ppermute | solution.py:337
  14.6 0.5 %collective-permute-start.3 = (s32[8,1,256]{2,1,0:T(1,128)S(1)}, s32[8,1,256]{2,1,0:T(1,128)S(1)}, u32[]{:S(2)}, u32[]{:S(2)}) collective-permute-start(s32[8,1,256]{2,1,0:T(1,128)S(1)} %pad_add_fusion), channel_id=1, source_target_pairs={{0,1},{1,0},{2,3},{3,2},{4,5},{5,4},{6,7},{7,6},{8,9},{9,8},{10,11... | collective-permute-start | bytes 24584 | tf_op jit(solution)/shard_map/ppermute | solution.py:337
  15.2 0.8 %collective-permute-done.3 = s32[8,1,256]{2,1,0:T(1,128)S(1)} collective-permute-done((s32[8,1,256]{2,1,0:T(1,128)S(1)}, s32[8,1,256]{2,1,0:T(1,128)S(1)}, u32[]{:S(2)}, u32[]{:S(2)}) %collective-permute-start.3) | collective-permute-done | bytes 8224 | tf_op jit(solution)/shard_map/ppermute | solution.py:337
  16.0 6.7 %probes.1 = f32[4,128,128]{2,1,0:T(8,128)} custom-call(s32[16,1,256]{2,1,0:T(1,128)S(1)} %constant_dynamic-update-slice_fusion.beam_ref, f32[4,2,16,128]{3,2,1,0:T(8,128)S(1)} %get-tuple-element.7.weight_ref, f32[2,512,256]{2,1,0:T(8,128)S(1)} %fetch.1.near_ref, bf16[4,2,512,256]{3,2,1,0:T(8,128)(2,1)S(1)} %get-tuple-element.8.right_ref, ...), custom_call_target="tpu_custom_call" | custom-call | tf_op jit(solution)/shard_map/probes/pallas_call | solution.py:306
  (8 shorter events, 0.0 us)
Async XLA Ops:
  0.7 7.6 %collective-permute-start = (s32[1,1,256]{2,1,0:T(1,128)S(1)}, s32[1,1,256]{2,1,0:T(1,128)S(1)}, u32[]{:S(2)}, u32[]{:S(2)}) collective-permute-start(s32[1,1,256]{2,1,0:T(1,128)S(1)} %bitcast.4), channel_id=1, source_target_pairs={{0,9},{1,8},{2,11},{3,10},{4,13},{5,12},{6,15},{7,14},{8,1},{9,0},... | collective-permute-start | bytes 3080 | tf_op jit(solution)/shard_map/ppermute | solution.py:337
  8.4 3.2 %collective-permute-start.1 = (s32[2,1,256]{2,1,0:T(1,128)S(1)}, s32[2,1,256]{2,1,0:T(1,128)S(1)}, u32[]{:S(2)}, u32[]{:S(2)}) collective-permute-start(s32[2,1,256]{2,1,0:T(1,128)S(1)} %pad_add_fusion.2), channel_id=1, source_target_pairs={{0,5},{1,4},{2,7},{3,6},{4,1},{5,0},{6,3},{7,2},{8,13},{9,12},{10,... | collective-permute-start | bytes 6152 | tf_op jit(solution)/shard_map/ppermute | solution.py:337
  11.6 3.0 %collective-permute-start.2 = (s32[4,1,256]{2,1,0:T(1,128)S(1)}, s32[4,1,256]{2,1,0:T(1,128)S(1)}, u32[]{:S(2)}, u32[]{:S(2)}) collective-permute-start(s32[4,1,256]{2,1,0:T(1,128)S(1)} %pad_add_fusion.1), channel_id=1, source_target_pairs={{0,3},{1,2},{2,1},{3,0},{4,7},{5,6},{6,5},{7,4},{8,11},{9,10},{10,... | collective-permute-start | bytes 12296 | tf_op jit(solution)/shard_map/ppermute | solution.py:337
  14.6 1.3 %collective-permute-start.3 = (s32[8,1,256]{2,1,0:T(1,128)S(1)}, s32[8,1,256]{2,1,0:T(1,128)S(1)}, u32[]{:S(2)}, u32[]{:S(2)}) collective-permute-start(s32[8,1,256]{2,1,0:T(1,128)S(1)} %pad_add_fusion), channel_id=1, source_target_pairs={{0,1},{1,0},{2,3},{3,2},{4,5},{5,4},{6,7},{7,6},{8,9},{9,8},{10,11... | collective-permute-start | bytes 24584 | tf_op jit(solution)/shard_map/ppermute | solution.py:337
